TPU v7x, 128 devices: a whole 4x4x4 slice. The times are simulated.
128 devices in a mesh: tile: 32 (over x, z, core), cuts: 4 (over y).
Axes of the slice: x: 4, y: 4, z: 4, core: 2. Of those that a mesh axis runs over, the one named last changes fastest.
Arguments:
- amplitudes: float32 [1024, 128, 128], P(('tile', 'cuts')), may hold values from 0 to 2
- positions: int32 [1024, 2], replicated, may hold values from 0 to 3968, as said below
- probe_field: float32 [2, 128, 128], replicated, may hold values from -4 to 4
- object_slices: float32 [4, 2, 256, 4096], P('cuts', None, None, 'tile'), may hold values from -1 to 1, as said below
Outputs:
- refined_object: float32 [4, 2, 256, 4096], P('cuts', None, None, 'tile')
Inputs may be any that keep to these rules, and one draw needn't show every extreme that they name: `positions`: rows lie in 0 .. 128; every frame's 128 columns lie inside the 4096 columns. A frame's owner tile is its column // 128. Frames are read in blocks of 8 consecutive frames, one block per device of tile+cuts in mesh order; one block holds at most 2 frames of any owner tile, and some block holds exactly 2. For every cuts index, the blocks of that index hold at most 16 frames of any one owner tile, and in every draw some owner tile receives exactly 16 from them. `object_slices`: transmissions have modulus at most 1.
All inputs are finite; a program needn't handle non-finite values.
Results may differ from a plain program's by a relative error of at most 0.015.
Values may be sent and summed in bfloat16 or wider, within the bound.
A program may use at most 128 MiB of HBM per device.

v0:
```python
import math
import jax
import jax.numpy as jnp
from jax import lax
from jax.sharding import PartitionSpec as P

ITERS = 2
STEP_SIZE = 0.05
AMPLITUDE_FLOOR = 0.25


def passed_along(x, axis, by):
    peers = lax.axis_size(axis)
    pairs = [(i, i + by) for i in range(peers) if 0 <= i + by < peers]
    return lax.ppermute(x, axis, pairs)


def block_table(real_part, imag_part):
    upper = jnp.stack([real_part, imag_part], axis=1)
    lower = jnp.stack([-imag_part, real_part], axis=1)
    return jnp.stack([upper, lower], axis=0).astype(jnp.bfloat16)


def make_tables(frame_side):
    highest = lax.Precision.HIGHEST
    index = jnp.arange(frame_side, dtype=jnp.int32)
    product = index[:, None] * index[None, :] % frame_side
    angle = product.astype(jnp.float32) * (2.0 * math.pi / frame_side)
    norm_scale = 1.0 / math.sqrt(frame_side)
    four_real = jnp.cos(angle) * norm_scale
    four_imag = -jnp.sin(angle) * norm_scale
    centred = (index + frame_side // 2) % frame_side - frame_side // 2
    chirp = -math.pi * (centred * centred).astype(jnp.float32) / (4.0 * frame_side)
    chirp_real = jnp.cos(chirp)
    chirp_imag = jnp.sin(chirp)
    left_real = four_real * chirp_real[None, :] + four_imag * chirp_imag[None, :]
    left_imag = four_real * chirp_imag[None, :] - four_imag * chirp_real[None, :]
    prop_real = jnp.dot(left_real, four_real, precision=highest) - jnp.dot(
        left_imag, four_imag, precision=highest
    )
    prop_imag = jnp.dot(left_real, four_imag, precision=highest) + jnp.dot(
        left_imag, four_real, precision=highest
    )
    return (
        block_table(four_real, four_imag),
        block_table(four_real, -four_imag),
        block_table(prop_real, prop_imag),
        block_table(prop_real, -prop_imag),
    )


def right_product(field, table):
    return jnp.einsum(
        "fcij,cjdk->fdik", field.astype(jnp.bfloat16), table, preferred_element_type=jnp.float32
    )


def two_sided(field, table):
    first = right_product(field, table)
    second = right_product(jnp.swapaxes(first, -1, -2), table)
    return jnp.swapaxes(second, -1, -2)


def complex_times(left, right):
    real_part = left[..., 0, :, :] * right[..., 0, :, :] - left[..., 1, :, :] * right[..., 1, :, :]
    imag_part = left[..., 0, :, :] * right[..., 1, :, :] + left[..., 1, :, :] * right[..., 0, :, :]
    return jnp.stack([real_part, imag_part], axis=-3)


def conj_times(left, right):
    real_part = left[..., 0, :, :] * right[..., 0, :, :] + left[..., 1, :, :] * right[..., 1, :, :]
    imag_part = left[..., 0, :, :] * right[..., 1, :, :] - left[..., 1, :, :] * right[..., 0, :, :]
    return jnp.stack([real_part, imag_part], axis=-3)


def frame_patches(windows, probe_field, measured, tables):
    four, four_conj, prop, prop_conj = tables
    slice_count = windows.shape[1]
    wave = complex_times(probe_field[None], windows[:, 0].astype(jnp.float32))
    fields = []
    for level in range(1, slice_count):
        moved = two_sided(wave, prop)
        fields.append(moved)
        wave = complex_times(windows[:, level].astype(jnp.float32), moved)
    far = two_sided(wave, four)
    magnitude = jnp.sqrt(far[:, 0] * far[:, 0] + far[:, 1] * far[:, 1])
    factor = 1.0 - measured / jnp.maximum(magnitude, AMPLITUDE_FLOOR)
    back = two_sided(far * factor[:, None], four_conj)
    patches = [None] * slice_count
    for level in range(slice_count - 1, 0, -1):
        patches[level] = conj_times(fields[level - 1], back)
        back = two_sided(conj_times(windows[:, level].astype(jnp.float32), back), prop_conj)
    patches[0] = conj_times(probe_field[None], back)
    return jnp.stack(patches, axis=1)


def cut_windows(panel, frame_rows, frame_cols, frame_side):
    zero_index = jnp.zeros((), jnp.int32)

    def window_at(row_start, col_start):
        start = (zero_index, zero_index, row_start, col_start)
        return lax.dynamic_slice(
            panel, start, (panel.shape[0], panel.shape[1], frame_side, frame_side)
        )

    return jax.vmap(window_at)(frame_rows, frame_cols)


def place_patches(panel_shape, patches, frame_rows, frame_cols, weights):
    panel_height = panel_shape[-2]
    panel_width = panel_shape[-1]
    frame_side = patches.shape[-1]
    offsets = jnp.arange(frame_side, dtype=jnp.int32)
    col_target = frame_cols[:, None] + offsets[None, :]
    col_onehot = (
        col_target[:, :, None] == jnp.arange(panel_width, dtype=jnp.int32)[None, None, :]
    ).astype(jnp.bfloat16)
    row_target = frame_rows[:, None] + offsets[None, :]
    row_onehot = (
        jnp.arange(panel_height, dtype=jnp.int32)[:, None, None] == row_target[None, :, :]
    ).astype(jnp.bfloat16)
    remain = patches * weights[:, None, None, None, None]
    gathered_sum = jnp.zeros(panel_shape, jnp.float32)
    for piece_index in range(3):
        piece_part = remain.astype(jnp.bfloat16)
        remain = remain - piece_part.astype(jnp.float32)
        placed_cols = jnp.einsum(
            "fscij,fjk->fscik", piece_part, col_onehot, preferred_element_type=jnp.float32
        ).astype(jnp.bfloat16)
        gathered_sum = gathered_sum + jnp.einsum(
            "hfi,fscik->schk", row_onehot, placed_cols, preferred_element_type=jnp.float32
        )
    return gathered_sum


def reduce_gradient(term_part):
    return lax.psum_scatter(term_part, "cuts", scatter_dimension=0, tiled=True)


def add_rim(main_part, moved_rim):
    extra = main_part.shape[-1] - moved_rim.shape[-1]
    return main_part + moved_rim


def body(amplitudes, positions, probe_field, object_slices):
    tile_count = lax.axis_size("tile")
    cut_count = lax.axis_size("cuts")
    tile_id = lax.axis_index("tile")
    cut_id = lax.axis_index("cuts")
    frame_side = probe_field.shape[-1]
    frames_held = amplitudes.shape[0]
    tile_width = object_slices.shape[-1]
    total_frames = positions.shape[0]
    reader_count = total_frames // frames_held
    capacity = max(2, 2 * frames_held // tile_count)
    max_load = 2 * frames_held
    row_list = positions[:, 0]
    col_list = positions[:, 1]
    owner = col_list // tile_width
    owner_grid = owner.reshape(reader_count, frames_held)
    earlier = jnp.tril(jnp.ones((frames_held, frames_held), jnp.int32), -1)
    same_owner = (owner_grid[:, :, None] == owner_grid[:, None, :]).astype(jnp.int32)
    slot_grid = jnp.sum(same_owner * earlier[None], axis=2)
    slot_list = slot_grid.reshape(total_frames)
    reader_self = tile_id * cut_count + cut_id
    my_owner = lax.dynamic_index_in_dim(owner_grid, reader_self, 0, keepdims=False)
    my_slot = lax.dynamic_index_in_dim(slot_grid, reader_self, 0, keepdims=False)
    target = my_owner * capacity + my_slot
    source = (
        jnp.full((tile_count * capacity,), frames_held, jnp.int32)
        .at[target]
        .set(jnp.arange(frames_held, dtype=jnp.int32))
    )
    padded = jnp.concatenate(
        [amplitudes, jnp.zeros((1, frame_side, frame_side), amplitudes.dtype)], axis=0
    )
    outgoing = jnp.take(padded, source, axis=0).reshape(
        tile_count, capacity, frame_side, frame_side
    )
    incoming = lax.all_to_all(outgoing, "tile", split_axis=0, concat_axis=0, tiled=True)
    reader_of = jnp.arange(total_frames, dtype=jnp.int32) // frames_held
    mine = (owner == tile_id) & (reader_of % cut_count == cut_id)
    rank_list = jnp.cumsum(mine.astype(jnp.int32)) - 1
    spot_list = jnp.where(mine, rank_list, max_load)
    chosen = (
        jnp.zeros((max_load,), jnp.int32)
        .at[spot_list]
        .set(jnp.arange(total_frames, dtype=jnp.int32), mode="drop")
    )
    live_weight = jnp.zeros((max_load,), jnp.float32).at[spot_list].set(1.0, mode="drop")
    flat_slot = reader_of // cut_count * capacity + slot_list
    picked = jnp.take(flat_slot, chosen)
    frames_in = jnp.take(
        incoming.reshape(tile_count * capacity, frame_side, frame_side), picked, axis=0
    )
    frame_rows = jnp.take(row_list, chosen)
    frame_cols = jnp.take(col_list, chosen) - tile_id * tile_width
    tables = make_tables(frame_side)
    current = object_slices
    for turn in range(ITERS):
        stacked = lax.all_gather(current.astype(jnp.bfloat16), "cuts", axis=0, tiled=True)
        next_rim = passed_along(stacked, "tile", -1)
        panel = jnp.concatenate([stacked, next_rim], axis=-1)
        windows = cut_windows(panel, frame_rows, frame_cols, frame_side)
        patches = frame_patches(windows, probe_field, frames_in, tables)
        term = place_patches(panel.shape, patches, frame_rows, frame_cols, live_weight)
        moved = passed_along(term[..., tile_width:], "tile", 1)
        share = reduce_gradient(add_rim(term[..., :tile_width], moved))
        current = current - STEP_SIZE * share
    return current


def solution(mesh):
    in_specs = (P(("tile", "cuts"), None, None), P(), P(), P("cuts", None, None, "tile"))
    out_specs = P("cuts", None, None, "tile")
    return jax.shard_map(body, mesh=mesh, in_specs=in_specs, out_specs=out_specs, check_vma=False)
```

profile of v0, /device:TPU:0, one launch (start us, length us, event | category | flops | bytes accessed | tf_op | source)
XLA Modules:
  0.0 458.6 jit_solution(10593045391714817191)
XLA Ops:
  7.5 13.4 %all_gather.6 = bf16[4,2,256,128]{3,2,1,0:T(8,128)(2,1)S(1)} all-gather(bf16[1,2,256,128]{3,2,1,0:T(8,128)(2,1)S(1)} %convert_element_type.304), channel_id=1, replica_groups=mesh['tile'=32,'cuts'=4] {'cuts'}, dimensions={0}, use_global_device_ids=true | all-gather | bytes 655360 | tf_op jit(solution)/shard_map/all_gather | solution.py:201
  29.6 4.5 broadcast_select_fusion
  34.1 9.0 %all-to-all-start = ((f32[32,2,128,128]{3,2,1,0:T(8,128)}), f32[32,2,128,128]{3,2,1,0:T(8,128)}, u32[]{:S(2)}, u32[]{:S(2)}) async-start(f32[32,2,128,128]{3,2,1,0:T(8,128)} %broadcast_select_fusion), calls=%async_computation | async-start | bytes 8388608 | tf_op jit(solution)/shard_map/all_to_all | solution.py:180
  44.9 4.3 scatter_custom_fusion
  52.8 4.8 %scatter_custom_fusion.2 = f32[16]{0:T(128)} fusion(s32[1024]{0:T(1024)S(1)} %bitcast.768, f32[1024]{0:T(1024)S(1)} %broadcast.687, f32[]{:T(128)} %constant.180.clone.1), kind=kCustom, calls=%fused_computation.444 | custom fusion | bytes 68 | tf_op jit(solution)/shard_map/scatter | solution.py:190
  62.3 44.7 %while.2 = (s32[]{:T(128)}, bf16[4,2,256,256]{3,2,1,0:T(8,128)(2,1)S(1)}, s32[16,4]{0,1:T(4,128)S(1)}, bf16[16,4,2,128,128]{4,3,2,0,1:T(8,128)(2,1)}, s32[]{:T(128)}) while((s32[]{:T(128)}, bf16[4,2,256,256]{3,2,1,0:T(8,128)(2,1)S(1)}, s32[16,4]{0,1:T(4,128)S(1)}, bf16[16,4,2,128,128]{4,3,2,0,1:T(8,128)(2,1)}, s32[]{:T(128)}) %tuple.101), condition=%wide.while_cond, body=%wide.while_body.sunk | while | flops 2 | bytes 525937 | solution.py:102
  107.1 5.1 %bitcast_convert_fusion.20 = (f32[16,2,128,128]{3,2,1,0:T(8,128)}, f32[16,2,128,128]{3,2,1,0:T(8,128)}, f32[16,2,128,128]{3,2,1,0:T(8,128)}, f32[16,2,128,128]{3,2,1,0:T(8,128)S(1)}) fusion(bf16[16,4,2,128,128]{4,3,2,0,1:T(8,128)(2,1)} %get-tuple-element.13), kind=kLoop, calls=%fused_computation.200 | loop fusion | flops 2097152 | bytes 12582912 | tf_op jit(solution)/shard_map/convert_element_type | solution.py:92
  133.5 4.1 convolution_bitcast_fusion.14
  137.7 5.4 %add_convert_fusion.9 = (bf16[16,1,128,128]{3,2,1,0:T(8,128)(2,1)}, bf16[16,1,128,128]{3,2,1,0:T(8,128)(2,1)}, f32[16,1,128,128]{3,2,1,0:T(8,128)}, f32[16,1,128,128]{3,2,1,0:T(8,128)}) fusion(f32[16,2,128,128]{3,2,1,0:T(8,128)} %convolution_bitcast_fusion.14, f32[16,2,128,128]{3,2,1,0:T(8,128)} %get-tuple-element.99, ...), kind=kLoop, calls=%fused_computation.251 | loop fusion | flops 3670016 | bytes 9437184 | tf_op jit(solution)/shard_map/convert.26
  143.1 3.3 convolution_bitcast_fusion.8
  146.4 5.4 %add_convert_fusion.8 = (bf16[16,1,128,128]{3,2,1,0:T(8,128)(2,1)}, bf16[16,1,128,128]{3,2,1,0:T(8,128)(2,1)}, f32[16,1,128,128]{3,2,1,0:T(8,128)}, f32[16,1,128,128]{3,2,1,0:T(8,128)}) fusion(f32[16,2,128,128]{3,2,1,0:T(8,128)} %convolution_bitcast_fusion.8, f32[16,2,128,128]{3,2,1,0:T(8,128)} %get-tuple-element.100, ...), kind=kLoop, calls=%fused_computation.249 | loop fusion | flops 3670016 | bytes 9437184 | tf_op jit(solution)/shard_map/convert.24
  155.2 4.7 %add_convert_fusion.7 = (bf16[16,1,128,128]{3,2,1,0:T(8,128)(2,1)}, bf16[16,1,128,128]{3,2,1,0:T(8,128)(2,1)}, f32[16,1,128,128]{3,2,1,0:T(8,128)}, f32[16,1,128,128]{3,2,1,0:T(8,128)}) fusion(f32[16,2,128,128]{3,2,1,0:T(8,128)} %convolution_bitcast_fusion.7, f32[16,2,128,128]{3,2,1,0:T(8,128)} %get-tuple-element.101, ...), kind=kLoop, calls=%fused_computation.247 | loop fusion | flops 3670016 | bytes 9437184 | tf_op jit(solution)/shard_map/convert.22
  167.4 6.4 %fusion.359 = (bf16[16,4,2,128,128]{4,3,2,0,1:T(8,128)(2,1)}, bf16[16,4,2,128,128]{4,3,2,0,1:T(8,128)(2,1)}, bf16[16,4,2,128,128]{4,3,2,0,1:T(8,128)(2,1)}) fusion(f32[16]{0:T(128)S(1)} %copy-done.22, f32[16,1,2,128,128]{4,3,2,0,1:T(8,128)S(1)} %maximum_bitcast_fusion.3, f32[16,1,2,128,128]{4,3,2,0,1:T(8,128)S(1)} %maximum_bitcast_fusion.2, ...), kind=kLoop, calls=%fused_computation.482 | loop fusion | flops 23068672 | bytes 20971584 | tf_op jit(solution)/shard_map/convert_element_type | solution.py:125
  173.8 8.1 %fusion.8 = f32[4,2,256,256,1]{3,2,4,1,0:T(8,128)} fusion(bf16[16,4,2,128,128]{4,3,2,0,1:T(8,128)(2,1)} %get-tuple-element.61, s32[16,128]{1,0:T(8,128)S(1)} %get-tuple-element.150, s32[16,128]{1,0:T(8,128)S(1)} %copy-done.19), kind=kOutput, calls=%fused_computation.25 | convolution fusion | flops 3226468352 | bytes 6307840 | tf_op jit(solution)/shard_map/hfi,fscik->schk/dot_general | solution.py:130
  181.9 8.2 %fusion.6 = f32[4,2,256,256,1]{3,2,4,1,0:T(8,128)} fusion(bf16[16,4,2,128,128]{4,3,2,0,1:T(8,128)(2,1)} %get-tuple-element.62, s32[16,128]{1,0:T(8,128)S(1)} %get-tuple-element.150, s32[16,128]{1,0:T(8,128)S(1)} %copy-done.19), kind=kOutput, calls=%fused_computation.22 | convolution fusion | flops 3226468352 | bytes 6307840 | tf_op jit(solution)/shard_map/hfi,fscik->schk/dot_general | solution.py:130
  190.1 8.3 %fusion.39 = f32[4,2,256,256]{2,3,1,0:T(8,128)S(1)} fusion(f32[4,2,256,256,1]{3,2,4,1,0:T(8,128)} %fusion.6, f32[4,2,256,256,1]{3,2,4,1,0:T(8,128)} %fusion.8, bf16[16,4,2,128,128]{4,3,2,0,1:T(8,128)(2,1)} %get-tuple-element.60, s32[16,128]{1,0:T(8,128)S(1)} %get-tuple-element.150, s32[16,128]{1,0:T(8,128)} %get-tuple-element.151), kind=kOutput, calls=%fused_computation.70 | convolution fusion | flops 3227516928 | bytes 10502144 | tf_op jit(solution)/shard_map/hfi,fscik->schk/dot_general | solution.py:130
  205.3 36.0 %reduce-scatter.3.cloned.1.call-done = f32[1,2,256,128]{2,3,1,0:T(8,128)} async-done(((f32[4,2,256,128]{2,3,1,0:T(8,128)}), f32[1,2,256,128]{2,3,1,0:T(8,128)}) %reduce-scatter.3.cloned.1.call-update) | async-done | bytes 262160 | tf_op jit(solution)/shard_map/reduce_scatter | solution.py:137
  242.4 12.8 %all_gather.7 = bf16[4,2,256,128]{3,2,1,0:T(8,128)(2,1)S(1)} all-gather(bf16[1,2,256,128]{3,2,1,0:T(8,128)(2,1)S(1)} %copy.237), channel_id=1, replica_groups=mesh['tile'=32,'cuts'=4] {'cuts'}, dimensions={0}, use_global_device_ids=true | all-gather | bytes 655360 | tf_op jit(solution)/shard_map/all_gather | solution.py:201
  262.1 46.3 %while.3 = (s32[]{:T(128)}, bf16[4,2,256,256]{3,2,1,0:T(8,128)(2,1)S(1)}, s32[16,4]{0,1:T(4,128)S(1)}, bf16[16,4,2,128,128]{4,3,2,0,1:T(8,128)(2,1)}, s32[]{:T(128)}) while((s32[]{:T(128)}, bf16[4,2,256,256]{3,2,1,0:T(8,128)(2,1)S(1)}, s32[16,4]{0,1:T(4,128)S(1)}, bf16[16,4,2,128,128]{4,3,2,0,1:T(8,128)(2,1)}, s32[]{:T(128)}) %tuple.111), condition=%wide.while_cond.1, body=%wide.while_body.1.sunk | while | flops 2 | bytes 525937 | solution.py:102
  308.4 5.2 %bitcast_convert_fusion.16 = (f32[16,2,128,128]{3,2,1,0:T(8,128)}, f32[16,2,128,128]{3,2,1,0:T(8,128)}, f32[16,2,128,128]{3,2,1,0:T(8,128)}, f32[16,2,128,128]{3,2,1,0:T(8,128)S(1)}) fusion(bf16[16,4,2,128,128]{4,3,2,0,1:T(8,128)(2,1)} %get-tuple-element.21), kind=kLoop, calls=%fused_computation.194 | loop fusion | flops 2097152 | bytes 12582912 | tf_op jit(solution)/shard_map/convert_element_type | solution.py:92
  323.0 3.5 subtract_convert_fusion.6
  329.9 3.6 subtract_convert_fusion.5
  339.9 3.9 convolution_bitcast_fusion.12
  343.8 5.0 %add_convert_fusion.2 = (bf16[16,1,128,128]{3,2,1,0:T(8,128)(2,1)}, bf16[16,1,128,128]{3,2,1,0:T(8,128)(2,1)}, f32[16,1,128,128]{3,2,1,0:T(8,128)S(1)}, f32[16,1,128,128]{3,2,1,0:T(8,128)}) fusion(f32[16,2,128,128]{3,2,1,0:T(8,128)} %convolution_bitcast_fusion.12, f32[16,2,128,128]{3,2,1,0:T(8,128)} %get-tuple-element.77, ...), kind=kLoop, calls=%fused_computation.217 | loop fusion | flops 3670016 | bytes 9437184 | tf_op jit(solution)/shard_map/convert.12
  352.1 5.4 %add_convert_fusion.1 = (bf16[16,1,128,128]{3,2,1,0:T(8,128)(2,1)}, bf16[16,1,128,128]{3,2,1,0:T(8,128)(2,1)}, f32[16,1,128,128]{3,2,1,0:T(8,128)}, f32[16,1,128,128]{3,2,1,0:T(8,128)}) fusion(f32[16,2,128,128]{3,2,1,0:T(8,128)} %convolution_bitcast_fusion.2, f32[16,2,128,128]{3,2,1,0:T(8,128)} %get-tuple-element.78, ...), kind=kLoop, calls=%fused_computation.215 | loop fusion | flops 3670016 | bytes 9437184 | tf_op jit(solution)/shard_map/convert.10
  360.8 4.6 %add_convert_fusion = (bf16[16,1,128,128]{3,2,1,0:T(8,128)(2,1)}, bf16[16,1,128,128]{3,2,1,0:T(8,128)(2,1)}, f32[16,1,128,128]{3,2,1,0:T(8,128)}, f32[16,1,128,128]{3,2,1,0:T(8,128)}) fusion(f32[16,2,128,128]{3,2,1,0:T(8,128)} %convolution_bitcast_fusion.1, f32[16,2,128,128]{3,2,1,0:T(8,128)} %get-tuple-element.79, ...), kind=kLoop, calls=%fused_computation.213 | loop fusion | flops 3670016 | bytes 9437184 | tf_op jit(solution)/shard_map/convert.8
  372.2 6.4 %fusion.358 = (bf16[16,4,2,128,128]{4,3,2,0,1:T(8,128)(2,1)}, bf16[16,4,2,128,128]{4,3,2,0,1:T(8,128)(2,1)}, bf16[16,4,2,128,128]{4,3,2,0,1:T(8,128)(2,1)}) fusion(f32[16]{0:T(128)S(1)} %copy-done.22, f32[16,1,2,128,128]{4,3,2,0,1:T(8,128)S(1)} %maximum_bitcast_fusion.7, f32[16,1,2,128,128]{4,3,2,0,1:T(8,128)S(1)} %maximum_bitcast_fusion.6, ...), kind=kLoop, calls=%fused_computation.481 | loop fusion | flops 23068672 | bytes 20971584 | tf_op jit(solution)/shard_map/convert_element_type | solution.py:125
  378.6 8.1 %fusion.2 = f32[4,2,256,256,1]{3,2,4,1,0:T(8,128)} fusion(bf16[16,4,2,128,128]{4,3,2,0,1:T(8,128)(2,1)} %get-tuple-element.58, s32[16,128]{1,0:T(8,128)S(1)} %get-tuple-element.150, s32[16,128]{1,0:T(8,128)S(1)} %copy-done.20), kind=kOutput, calls=%fused_computation.17 | convolution fusion | flops 3226468352 | bytes 6307840 | tf_op jit(solution)/shard_map/hfi,fscik->schk/dot_general | solution.py:130
  386.8 8.2 %fusion = f32[4,2,256,256,1]{3,2,4,1,0:T(8,128)} fusion(bf16[16,4,2,128,128]{4,3,2,0,1:T(8,128)(2,1)} %get-tuple-element.59, s32[16,128]{1,0:T(8,128)S(1)} %get-tuple-element.150, s32[16,128]{1,0:T(8,128)S(1)} %copy-done.20), kind=kOutput, calls=%fused_computation.14 | convolution fusion | flops 3226468352 | bytes 6307840 | tf_op jit(solution)/shard_map/hfi,fscik->schk/dot_general | solution.py:130
  395.0 8.4 %fusion.38 = f32[4,2,256,256]{2,3,1,0:T(8,128)S(1)} fusion(f32[4,2,256,256,1]{3,2,4,1,0:T(8,128)} %fusion, f32[4,2,256,256,1]{3,2,4,1,0:T(8,128)} %fusion.2, bf16[16,4,2,128,128]{4,3,2,0,1:T(8,128)(2,1)} %get-tuple-element.57, s32[16,128]{1,0:T(8,128)S(1)} %get-tuple-element.150, s32[16,128]{1,0:T(8,128)S(1)} %copy-done.20), kind=kOutput, calls=%fused_computation.65 | convolution fusion | flops 3227516928 | bytes 10502144 | tf_op jit(solution)/shard_map/hfi,fscik->schk/dot_general | solution.py:130
  403.5 8.7 %collective-permute-start.3 = (f32[4,2,256,128]{2,3,1,0:T(8,128)S(1)}, f32[4,2,256,128]{2,3,1,0:T(8,128)S(1)}, u32[]{:S(2)}, u32[]{:S(2)}) collective-permute-start(f32[4,2,256,128]{2,3,1,0:T(8,128)S(1)} %slice.507), channel_id=1, source_target_pairs={{0,4},{4,8},{8,12},{12,16},{16,20},{20,24},{24,28},{28,32},{32,36}... | collective-permute-start | bytes 3145736 | tf_op jit(solution)/shard_map/ppermute | solution.py:15
  415.6 33.9 %reduce-scatter.5.cloned.1.call-done = f32[1,2,256,128]{2,3,1,0:T(8,128)} async-done(((f32[4,2,256,128]{2,3,1,0:T(8,128)}), f32[1,2,256,128]{2,3,1,0:T(8,128)}) %reduce-scatter.5.cloned.1.call-update) | async-done | bytes 262160 | tf_op jit(solution)/shard_map/reduce_scatter | solution.py:137
  (251 shorter events, 195.0 us)
Async XLA Ops:
  20.9 38.2 %collective-permute-start = (bf16[4,2,256,128]{3,2,1,0:T(8,128)(2,1)S(1)}, bf16[4,2,256,128]{3,2,1,0:T(8,128)(2,1)S(1)}, u32[]{:S(2)}, u32[]{:S(2)}) collective-permute-start(bf16[4,2,256,128]{3,2,1,0:T(8,128)(2,1)S(1)} %all_gather.6), channel_id=1, source_target_pairs={{4,0},{8,4},{12,8},{16,12},{20,16},{24,20},{28,24},{32,28},{36,32}... | collective-permute-start | bytes 1572872 | tf_op jit(solution)/shard_map/ppermute | solution.py:15
  34.1 93.5 %all-to-all-start = ((f32[32,2,128,128]{3,2,1,0:T(8,128)}), f32[32,2,128,128]{3,2,1,0:T(8,128)}, u32[]{:S(2)}, u32[]{:S(2)}) async-start(f32[32,2,128,128]{3,2,1,0:T(8,128)} %broadcast_select_fusion), calls=%async_computation | async-start | bytes 8388608 | tf_op jit(solution)/shard_map/all_to_all | solution.py:180
  43.1 198.1 %reduce-scatter.3.cloned.1.call-start = ((), (), s32[]{:S(2)}) async-start(), calls=%async_computation.3 | async-start | bytes 1310720 | tf_op jit(solution)/shard_map/reduce_scatter | solution.py:137
  43.8 15.3 %copy-start.18 = (f32[2,128,128]{2,1,0:T(8,128)S(1)}, f32[2,128,128]{2,1,0:T(8,128)}, u32[]{:S(2)}) copy-start(f32[2,128,128]{2,1,0:T(8,128)} %param.8) | copy-start | bytes 393220
  162.1 1.2 copy-start.9
  162.1 1.5 copy-start.10
  163.6 1.2 copy-start.5
  163.6 1.5 copy-start.6
  165.2 1.2 copy-start.1
  165.2 1.5 copy-start.2
  166.7 0.7 copy-start.22
  167.4 6.4 %copy-start.19 = (s32[16,128]{1,0:T(8,128)S(1)}, s32[16,128]{1,0:T(8,128)}, u32[]{:S(2)}) copy-start(s32[16,128]{1,0:T(8,128)} %get-tuple-element.151) | copy-start | bytes 24580
  198.6 4.4 collective-permute-start.1
  204.1 245.3 %reduce-scatter.5.cloned.1.call-start = ((), (), s32[]{:S(2)}) async-start(), calls=%async_computation.4 | async-start | bytes 1310720 | tf_op jit(solution)/shard_map/reduce_scatter | solution.py:137
  205.3 51.2 %copy-start.11 = (f32[1,2,256,128]{2,3,1,0:T(8,128)}, f32[1,2,256,128]{2,3,1,0:T(8,128)S(1)}, u32[]{:S(2)}) copy-start(f32[1,2,256,128]{2,3,1,0:T(8,128)S(1)} %copy.236) | copy-start | bytes 786436
  255.2 3.8 collective-permute-start.2
  329.9 3.6 copy-start.15
  329.9 3.6 copy-start.16
  333.4 3.3 copy-start.21
  336.8 3.1 copy-start.13
  336.8 3.1 copy-start.14
  367.7 1.2 copy-start.7
  367.7 1.5 copy-start.8
  369.2 1.2 copy-start.3
  369.2 1.5 copy-start.4
  370.8 1.2 copy-start
  372.2 6.4 %copy-start.20 = (s32[16,128]{1,0:T(8,128)S(1)}, s32[16,128]{1,0:T(8,128)}, u32[]{:S(2)}) copy-start(s32[16,128]{1,0:T(8,128)} %get-tuple-element.151) | copy-start | bytes 24580
  403.5 46.0 %copy-start.12 = (f32[1,2,256,128]{2,3,1,0:T(8,128)S(1)}, f32[1,2,256,128]{2,3,1,0:T(8,128)}, u32[]{:S(2)}) copy-start(f32[1,2,256,128]{2,3,1,0:T(8,128)} %copy-done.11) | copy-start | bytes 786436
  403.5 46.0 %copy-start.17 = (f32[1,2,256,128]{2,3,1,0:T(8,128)S(1)}, f32[1,2,256,128]{2,3,1,0:T(8,128)}, u32[]{:S(2)}) copy-start(f32[1,2,256,128]{2,3,1,0:T(8,128)} %reduce-scatter.3.cloned.1.call-done) | copy-start | bytes 786436
  403.5 10.9 %collective-permute-start.3 = (f32[4,2,256,128]{2,3,1,0:T(8,128)S(1)}, f32[4,2,256,128]{2,3,1,0:T(8,128)S(1)}, u32[]{:S(2)}, u32[]{:S(2)}) collective-permute-start(f32[4,2,256,128]{2,3,1,0:T(8,128)S(1)} %slice.507), channel_id=1, source_target_pairs={{0,4},{4,8},{8,12},{12,16},{16,20},{20,24},{24,28},{28,32},{32,36}... | collective-permute-start | bytes 3145736 | tf_op jit(solution)/shard_map/ppermute | solution.py:15
Sparse Core Ops, SparseCore 0:
  204.3 36.9 reduce-scatter.2
  415.7 33.6 reduce-scatter.4
where the time goes:
time: 466 us; the launch traced here: 459 us
  local copies, waits for them, and re-layouts  127 us (27%)
  matrix products  96.5 us (21%)
  other arithmetic  95.2 us (20%)
  waiting for transfers between devices  76.8 us (16%)
  blocking collectives  26.2 us (6%)
  starting transfers between devices  22.6 us (5%)
  between operations  14.4 us (3%)
    gather x96, local copies, waits for them, and re-layouts  90.8 us
    reduce_scatter x2, waiting for transfers between devices, reduce_gradient(): return lax.psum_scatter(term_part, 'cuts', scatter_dimension=0, tiled=True)  69.8 us
    another operation x18, other arithmetic  50.1 us
    dot_general x6, matrix products, place_patches(): jnp.einsum('hfi,fscik->schk', row_onehot, placed_cols, preferred_element_...  49.4 us
    dot_general x16, matrix products, right_product(): jnp.einsum('fcij,cjdk->fdik', field.astype(jnp.bfloat16), table, preferre...  45.2 us
    all_gather x2, blocking collectives, body(): lax.all_gather(current.astype(jnp.bfloat16), 'cuts', axis=0, tiled=True)  26.2 us
    unnamed x49, local copies, waits for them, and re-layouts  15.1 us
    ppermute x4, starting transfers between devices, passed_along(): return lax.ppermute(x, axis, pairs)  13.5 us
  transfers between devices with their start and end apart: 7, of which 5 were waited for; matrix products, arithmetic and copies ran while one was open for 21% of the time, Pallas kernels for 0%

commit v1 on v0

--- a/solution.py
+++ b/solution.py
@@ -198,7 +198,12 @@
     tables = make_tables(frame_side)
     current = object_slices
     for turn in range(ITERS):
-        stacked = lax.all_gather(current.astype(jnp.bfloat16), "cuts", axis=0, tiled=True)
+        stacked = jnp.concatenate(
+            lax.all_to_all(
+                jnp.stack([current.astype(jnp.bfloat16)] * lax.axis_size("cuts"), 0), "cuts", 0, 0
+            ),
+            axis=0,
+        )
         next_rim = passed_along(stacked, "tile", -1)
         panel = jnp.concatenate([stacked, next_rim], axis=-1)
         windows = cut_windows(panel, frame_rows, frame_cols, frame_side)

time: 466 us -> 505 us (1.084)
  starting transfers between devices: 22.6 us -> 78.2 us
  blocking collectives: 26.2 us -> 10.7 us
    ppermute x4, starting transfers between devices: 13.5 us -> 65.1 us  [passed_along(): return lax.ppermute(x, axis, pairs)]
    all_gather x2 -> x0, blocking collectives: 26.2 us -> none  [body(): lax.all_gather(current.astype(jnp.bfloat16), 'cuts', axis=0, tiled=True)]
    all_to_all x0 -> x1, blocking collectives: none -> 10.7 us  [body(): lax.all_to_all(jnp.stack([current.astype(jnp.bfloat16)] * lax.axis_size('...]
    unnamed x49 -> x53, local copies, waits for them, and re-layouts: 15.1 us -> 15.1 us
  transfers between devices with their start and end apart: 7 -> 8, of which waited for: 5 -> 6; matrix products, arithmetic and copies ran while one was open for 21% -> 19% of each run, Pallas kernels for 0% -> 0%
where the time goes in v1:
time: 505 us; the launch traced here: 497 us
  local copies, waits for them, and re-layouts  126 us (25%)
  matrix products  96.4 us (19%)
  other arithmetic  94.5 us (19%)
  starting transfers between devices  78.2 us (15%)
  waiting for transfers between devices  76.3 us (15%)
  between operations  14.4 us (3%)
  blocking collectives  10.7 us (2%)
    gather x96, local copies, waits for them, and re-layouts  91 us
    reduce_scatter x2, waiting for transfers between devices, reduce_gradient(): return lax.psum_scatter(term_part, 'cuts', scatter_dimension=0, tiled=True)  67.6 us
    ppermute x4, starting transfers between devices, passed_along(): return lax.ppermute(x, axis, pairs)  65.1 us
    another operation x18, other arithmetic  50.2 us
    dot_general x6, matrix products, place_patches(): jnp.einsum('hfi,fscik->schk', row_onehot, placed_cols, preferred_element_...  49.3 us
    dot_general x16, matrix products, right_product(): jnp.einsum('fcij,cjdk->fdik', field.astype(jnp.bfloat16), table, preferre...  45.2 us
    unnamed x53, local copies, waits for them, and re-layouts  15.1 us
    convert_element_type x2, other arithmetic, place_patches(): piece_part = remain.astype(jnp.bfloat16)  12.7 us
  transfers between devices with their start and end apart: 8, of which 6 were waited for; matrix products, arithmetic and copies ran while one was open for 19% of the time, Pallas kernels for 0%

profile of v1, /device:TPU:0, one launch (start us, length us, event | category | flops | bytes accessed | tf_op | source)
XLA Modules:
  0.0 497.1 jit_solution(233483592203872304)
XLA Ops:
  8.4 4.6 all-to-all-start
  16.6 4.3 scatter_custom_fusion
  24.7 4.8 scatter_custom_fusion.2
  33.1 4.5 broadcast_select_fusion
  37.6 8.4 %all-to-all-start.1 = ((f32[32,2,128,128]{3,2,1,0:T(8,128)}), f32[32,2,128,128]{3,2,1,0:T(8,128)}, u32[]{:S(2)}, u32[]{:S(2)}) async-start(f32[32,2,128,128]{3,2,1,0:T(8,128)} %broadcast_select_fusion), calls=%async_computation.1 | async-start | bytes 8388608 | tf_op jit(solution)/shard_map/all_to_all | solution.py:180
  53.1 44.5 %while.2 = (s32[]{:T(128)}, bf16[4,2,256,256]{3,2,1,0:T(8,128)(2,1)S(1)}, s32[16,4]{0,1:T(4,128)S(1)}, bf16[16,4,2,128,128]{4,3,2,0,1:T(8,128)(2,1)}, s32[]{:T(128)}) while((s32[]{:T(128)}, bf16[4,2,256,256]{3,2,1,0:T(8,128)(2,1)S(1)}, s32[16,4]{0,1:T(4,128)S(1)}, bf16[16,4,2,128,128]{4,3,2,0,1:T(8,128)(2,1)}, s32[]{:T(128)}) %tuple.99), condition=%wide.while_cond, body=%wide.while_body.sunk | while | flops 2 | bytes 525937 | solution.py:102
  97.7 5.1 %bitcast_convert_fusion.20 = (f32[16,2,128,128]{3,2,1,0:T(8,128)}, f32[16,2,128,128]{3,2,1,0:T(8,128)}, f32[16,2,128,128]{3,2,1,0:T(8,128)}, f32[16,2,128,128]{3,2,1,0:T(8,128)S(1)}) fusion(bf16[16,4,2,128,128]{4,3,2,0,1:T(8,128)(2,1)} %get-tuple-element.13), kind=kLoop, calls=%fused_computation.200 | loop fusion | flops 2097152 | bytes 12582912 | tf_op jit(solution)/shard_map/convert_element_type | solution.py:92
  124.1 4.1 convolution_bitcast_fusion.14
  128.2 5.5 %add_convert_fusion.9 = (bf16[16,1,128,128]{3,2,1,0:T(8,128)(2,1)}, bf16[16,1,128,128]{3,2,1,0:T(8,128)(2,1)}, f32[16,1,128,128]{3,2,1,0:T(8,128)}, f32[16,1,128,128]{3,2,1,0:T(8,128)}) fusion(f32[16,2,128,128]{3,2,1,0:T(8,128)} %convolution_bitcast_fusion.14, f32[16,2,128,128]{3,2,1,0:T(8,128)} %get-tuple-element.91, ...), kind=kLoop, calls=%fused_computation.251 | loop fusion | flops 3670016 | bytes 9437184 | tf_op jit(solution)/shard_map/convert.26
  137.0 5.4 %add_convert_fusion.8 = (bf16[16,1,128,128]{3,2,1,0:T(8,128)(2,1)}, bf16[16,1,128,128]{3,2,1,0:T(8,128)(2,1)}, f32[16,1,128,128]{3,2,1,0:T(8,128)}, f32[16,1,128,128]{3,2,1,0:T(8,128)}) fusion(f32[16,2,128,128]{3,2,1,0:T(8,128)} %convolution_bitcast_fusion.8, f32[16,2,128,128]{3,2,1,0:T(8,128)} %get-tuple-element.92, ...), kind=kLoop, calls=%fused_computation.249 | loop fusion | flops 3670016 | bytes 9437184 | tf_op jit(solution)/shard_map/convert.24
  145.8 4.7 add_convert_fusion.7
  158.0 6.4 %fusion.358 = (bf16[16,4,2,128,128]{4,3,2,0,1:T(8,128)(2,1)}, bf16[16,4,2,128,128]{4,3,2,0,1:T(8,128)(2,1)}, bf16[16,4,2,128,128]{4,3,2,0,1:T(8,128)(2,1)}) fusion(f32[16]{0:T(128)S(1)} %copy-done.24, f32[16,1,2,128,128]{4,3,2,0,1:T(8,128)S(1)} %maximum_bitcast_fusion.3, f32[16,1,2,128,128]{4,3,2,0,1:T(8,128)S(1)} %maximum_bitcast_fusion.2, ...), kind=kLoop, calls=%fused_computation.483 | loop fusion | flops 23068672 | bytes 20971584 | tf_op jit(solution)/shard_map/convert_element_type | solution.py:125
  164.4 8.1 %fusion.8 = f32[4,2,256,256,1]{3,2,4,1,0:T(8,128)} fusion(bf16[16,4,2,128,128]{4,3,2,0,1:T(8,128)(2,1)} %get-tuple-element.53, s32[16,128]{1,0:T(8,128)S(1)} %get-tuple-element.142, s32[16,128]{1,0:T(8,128)S(1)} %copy-done.21), kind=kOutput, calls=%fused_computation.25 | convolution fusion | flops 3226468352 | bytes 6307840 | tf_op jit(solution)/shard_map/hfi,fscik->schk/dot_general | solution.py:130
  172.5 8.2 %fusion.6 = f32[4,2,256,256,1]{3,2,4,1,0:T(8,128)} fusion(bf16[16,4,2,128,128]{4,3,2,0,1:T(8,128)(2,1)} %get-tuple-element.54, s32[16,128]{1,0:T(8,128)S(1)} %get-tuple-element.142, s32[16,128]{1,0:T(8,128)S(1)} %copy-done.21), kind=kOutput, calls=%fused_computation.22 | convolution fusion | flops 3226468352 | bytes 6307840 | tf_op jit(solution)/shard_map/hfi,fscik->schk/dot_general | solution.py:130
  180.7 8.3 %fusion.39 = f32[4,2,256,256]{2,3,1,0:T(8,128)S(1)} fusion(f32[4,2,256,256,1]{3,2,4,1,0:T(8,128)} %fusion.6, f32[4,2,256,256,1]{3,2,4,1,0:T(8,128)} %fusion.8, bf16[16,4,2,128,128]{4,3,2,0,1:T(8,128)(2,1)} %get-tuple-element.52, s32[16,128]{1,0:T(8,128)S(1)} %get-tuple-element.142, s32[16,128]{1,0:T(8,128)} %get-tuple-element.143), kind=kOutput, calls=%fused_computation.70 | convolution fusion | flops 3227516928 | bytes 10502144 | tf_op jit(solution)/shard_map/hfi,fscik->schk/dot_general | solution.py:130
  189.1 53.9 %collective-permute-start.1 = (f32[4,2,256,128]{2,3,1,0:T(8,128)S(1)}, f32[4,2,256,128]{2,3,1,0:T(8,128)S(1)}, u32[]{:S(2)}, u32[]{:S(2)}) collective-permute-start(f32[4,2,256,128]{2,3,1,0:T(8,128)S(1)} %slice.481), channel_id=1, source_target_pairs={{0,4},{4,8},{8,12},{12,16},{16,20},{20,24},{24,28},{28,32},{32,36}... | collective-permute-start | bytes 3145736 | tf_op jit(solution)/shard_map/ppermute | solution.py:15
  247.6 34.0 %reduce-scatter.3.cloned.1.call-done = f32[1,2,256,128]{2,3,1,0:T(8,128)} async-done(((f32[4,2,256,128]{2,3,1,0:T(8,128)}), f32[1,2,256,128]{2,3,1,0:T(8,128)}) %reduce-scatter.3.cloned.1.call-update) | async-done | bytes 262160 | tf_op jit(solution)/shard_map/reduce_scatter | solution.py:137
  282.8 10.7 %all_to_all.15 = bf16[4,1,2,256,128]{4,3,2,1,0:T(8,128)(2,1)S(1)} all-to-all(bf16[4,1,2,256,128]{4,3,2,1,0:T(8,128)(2,1)S(1)} %stack.310), channel_id=1, replica_groups=mesh['tile'=32,'cuts'=4] {'cuts'}, dimensions={0} | all-to-all | bytes 1048576 | tf_op jit(solution)/shard_map/all_to_all | solution.py:202
  300.4 46.7 %while.3 = (s32[]{:T(128)}, bf16[4,2,256,256]{3,2,1,0:T(8,128)(2,1)S(1)}, s32[16,4]{0,1:T(4,128)S(1)}, bf16[16,4,2,128,128]{4,3,2,0,1:T(8,128)(2,1)}, s32[]{:T(128)}) while((s32[]{:T(128)}, bf16[4,2,256,256]{3,2,1,0:T(8,128)(2,1)S(1)}, s32[16,4]{0,1:T(4,128)S(1)}, bf16[16,4,2,128,128]{4,3,2,0,1:T(8,128)(2,1)}, s32[]{:T(128)}) %tuple.109), condition=%wide.while_cond.1, body=%wide.while_body.1.sunk | while | flops 2 | bytes 525937 | solution.py:102
  347.1 5.2 %bitcast_convert_fusion.16 = (f32[16,2,128,128]{3,2,1,0:T(8,128)}, f32[16,2,128,128]{3,2,1,0:T(8,128)}, f32[16,2,128,128]{3,2,1,0:T(8,128)}, f32[16,2,128,128]{3,2,1,0:T(8,128)S(1)}) fusion(bf16[16,4,2,128,128]{4,3,2,0,1:T(8,128)(2,1)} %get-tuple-element.21), kind=kLoop, calls=%fused_computation.194 | loop fusion | flops 2097152 | bytes 12582912 | tf_op jit(solution)/shard_map/convert_element_type | solution.py:92
  361.8 3.5 subtract_convert_fusion.6
  368.7 3.6 subtract_convert_fusion.5
  378.7 3.9 convolution_bitcast_fusion.12
  382.6 5.0 %add_convert_fusion.2 = (bf16[16,1,128,128]{3,2,1,0:T(8,128)(2,1)}, bf16[16,1,128,128]{3,2,1,0:T(8,128)(2,1)}, f32[16,1,128,128]{3,2,1,0:T(8,128)S(1)}, f32[16,1,128,128]{3,2,1,0:T(8,128)}) fusion(f32[16,2,128,128]{3,2,1,0:T(8,128)} %convolution_bitcast_fusion.12, f32[16,2,128,128]{3,2,1,0:T(8,128)} %get-tuple-element.69, ...), kind=kLoop, calls=%fused_computation.217 | loop fusion | flops 3670016 | bytes 9437184 | tf_op jit(solution)/shard_map/convert.12
  390.9 5.4 %add_convert_fusion.1 = (bf16[16,1,128,128]{3,2,1,0:T(8,128)(2,1)}, bf16[16,1,128,128]{3,2,1,0:T(8,128)(2,1)}, f32[16,1,128,128]{3,2,1,0:T(8,128)}, f32[16,1,128,128]{3,2,1,0:T(8,128)}) fusion(f32[16,2,128,128]{3,2,1,0:T(8,128)} %convolution_bitcast_fusion.2, f32[16,2,128,128]{3,2,1,0:T(8,128)} %get-tuple-element.70, ...), kind=kLoop, calls=%fused_computation.215 | loop fusion | flops 3670016 | bytes 9437184 | tf_op jit(solution)/shard_map/convert.10
  399.7 4.6 add_convert_fusion
  411.1 6.4 %fusion.357 = (bf16[16,4,2,128,128]{4,3,2,0,1:T(8,128)(2,1)}, bf16[16,4,2,128,128]{4,3,2,0,1:T(8,128)(2,1)}, bf16[16,4,2,128,128]{4,3,2,0,1:T(8,128)(2,1)}) fusion(f32[16]{0:T(128)S(1)} %copy-done.24, f32[16,1,2,128,128]{4,3,2,0,1:T(8,128)S(1)} %maximum_bitcast_fusion.7, f32[16,1,2,128,128]{4,3,2,0,1:T(8,128)S(1)} %maximum_bitcast_fusion.6, ...), kind=kLoop, calls=%fused_computation.482 | loop fusion | flops 23068672 | bytes 20971584 | tf_op jit(solution)/shard_map/convert_element_type | solution.py:125
  417.5 8.1 %fusion.2 = f32[4,2,256,256,1]{3,2,4,1,0:T(8,128)} fusion(bf16[16,4,2,128,128]{4,3,2,0,1:T(8,128)(2,1)} %get-tuple-element.50, s32[16,128]{1,0:T(8,128)S(1)} %get-tuple-element.142, s32[16,128]{1,0:T(8,128)S(1)} %copy-done.22), kind=kOutput, calls=%fused_computation.17 | convolution fusion | flops 3226468352 | bytes 6307840 | tf_op jit(solution)/shard_map/hfi,fscik->schk/dot_general | solution.py:130
  425.6 8.2 %fusion = f32[4,2,256,256,1]{3,2,4,1,0:T(8,128)} fusion(bf16[16,4,2,128,128]{4,3,2,0,1:T(8,128)(2,1)} %get-tuple-element.51, s32[16,128]{1,0:T(8,128)S(1)} %get-tuple-element.142, s32[16,128]{1,0:T(8,128)S(1)} %copy-done.22), kind=kOutput, calls=%fused_computation.14 | convolution fusion | flops 3226468352 | bytes 6307840 | tf_op jit(solution)/shard_map/hfi,fscik->schk/dot_general | solution.py:130
  433.8 8.4 %fusion.38 = f32[4,2,256,256]{2,3,1,0:T(8,128)S(1)} fusion(f32[4,2,256,256,1]{3,2,4,1,0:T(8,128)} %fusion, f32[4,2,256,256,1]{3,2,4,1,0:T(8,128)} %fusion.2, bf16[16,4,2,128,128]{4,3,2,0,1:T(8,128)(2,1)} %get-tuple-element.49, s32[16,128]{1,0:T(8,128)S(1)} %get-tuple-element.142, s32[16,128]{1,0:T(8,128)S(1)} %copy-done.22), kind=kOutput, calls=%fused_computation.65 | convolution fusion | flops 3227516928 | bytes 10502144 | tf_op jit(solution)/shard_map/hfi,fscik->schk/dot_general | solution.py:130
  442.3 8.7 %collective-permute-start.3 = (f32[4,2,256,128]{2,3,1,0:T(8,128)S(1)}, f32[4,2,256,128]{2,3,1,0:T(8,128)S(1)}, u32[]{:S(2)}, u32[]{:S(2)}) collective-permute-start(f32[4,2,256,128]{2,3,1,0:T(8,128)S(1)} %slice.507), channel_id=1, source_target_pairs={{0,4},{4,8},{8,12},{12,16},{16,20},{20,24},{24,28},{28,32},{32,36}... | collective-permute-start | bytes 3145736 | tf_op jit(solution)/shard_map/ppermute | solution.py:15
  454.4 33.6 %reduce-scatter.5.cloned.1.call-done = f32[1,2,256,128]{2,3,1,0:T(8,128)} async-done(((f32[4,2,256,128]{2,3,1,0:T(8,128)}), f32[1,2,256,128]{2,3,1,0:T(8,128)}) %reduce-scatter.5.cloned.1.call-update) | async-done | bytes 262160 | tf_op jit(solution)/shard_map/reduce_scatter | solution.py:137
  (258 shorter events, 196.7 us)
Async XLA Ops:
  6.5 8.1 %copy-start.20 = (s32[1024,2]{0,1:T(2,128)S(1)}, s32[1024,2]{0,1:T(2,128)}, u32[]{:S(2)}) copy-start(s32[1024,2]{0,1:T(2,128)} %param.7) | copy-start | bytes 24580
  8.4 29.2 %all-to-all-start = ((bf16[4,1,2,256,128]{4,3,2,1,0:T(8,128)(2,1)}), bf16[4,1,2,256,128]{4,3,2,1,0:T(8,128)(2,1)S(1)}, u32[]{:S(2)}, u32[]{:S(2)}) async-start(bf16[4,1,2,256,128]{4,3,2,1,0:T(8,128)(2,1)} %stack.278), calls=%async_computation | async-start | bytes 1048576 | tf_op jit(solution)/shard_map/all_to_all | solution.py:202
  13.5 11.1 %copy-start.18 = (f32[8,128,128]{2,1,0:T(8,128)S(1)}, f32[8,128,128]{2,1,0:T(8,128)}, u32[]{:S(2)}) copy-start(f32[8,128,128]{2,1,0:T(8,128)} %param.6) | copy-start | bytes 1572868
  37.6 10.5 %copy-start.19 = (f32[2,128,128]{2,1,0:T(8,128)S(1)}, f32[2,128,128]{2,1,0:T(8,128)}, u32[]{:S(2)}) copy-start(f32[2,128,128]{2,1,0:T(8,128)} %param.8) | copy-start | bytes 393220
  37.6 80.6 %all-to-all-start.1 = ((f32[32,2,128,128]{3,2,1,0:T(8,128)}), f32[32,2,128,128]{3,2,1,0:T(8,128)}, u32[]{:S(2)}, u32[]{:S(2)}) async-start(f32[32,2,128,128]{3,2,1,0:T(8,128)} %broadcast_select_fusion), calls=%async_computation.1 | async-start | bytes 8388608 | tf_op jit(solution)/shard_map/all_to_all | solution.py:180
  46.1 235.5 %reduce-scatter.3.cloned.1.call-start = ((), (), s32[]{:S(2)}) async-start(), calls=%async_computation.5 | async-start | bytes 1310720 | tf_op jit(solution)/shard_map/reduce_scatter | solution.py:137
  46.1 3.8 collective-permute-start
  152.7 1.2 copy-start.9
  152.7 1.5 copy-start.10
  154.3 1.2 copy-start.5
  154.3 1.5 copy-start.6
  155.8 1.2 copy-start.1
  155.8 1.5 copy-start.2
  158.0 6.4 %copy-start.21 = (s32[16,128]{1,0:T(8,128)S(1)}, s32[16,128]{1,0:T(8,128)}, u32[]{:S(2)}) copy-start(s32[16,128]{1,0:T(8,128)} %get-tuple-element.143) | copy-start | bytes 24580
  189.1 56.1 %collective-permute-start.1 = (f32[4,2,256,128]{2,3,1,0:T(8,128)S(1)}, f32[4,2,256,128]{2,3,1,0:T(8,128)S(1)}, u32[]{:S(2)}, u32[]{:S(2)}) collective-permute-start(f32[4,2,256,128]{2,3,1,0:T(8,128)S(1)} %slice.481), channel_id=1, source_target_pairs={{0,4},{4,8},{8,12},{12,16},{16,20},{20,24},{24,28},{28,32},{32,36}... | collective-permute-start | bytes 3145736 | tf_op jit(solution)/shard_map/ppermute | solution.py:15
  246.4 241.6 %reduce-scatter.5.cloned.1.call-start = ((), (), s32[]{:S(2)}) async-start(), calls=%async_computation.6 | async-start | bytes 1310720 | tf_op jit(solution)/shard_map/reduce_scatter | solution.py:137
  247.5 47.2 %copy-start.11 = (f32[1,2,256,128]{2,3,1,0:T(8,128)}, f32[1,2,256,128]{2,3,1,0:T(8,128)S(1)}, u32[]{:S(2)}) copy-start(f32[1,2,256,128]{2,3,1,0:T(8,128)S(1)} %copy.236) | copy-start | bytes 786436
  293.5 3.8 collective-permute-start.2
  368.7 3.6 copy-start.15
  368.7 3.6 copy-start.16
  372.3 3.3 copy-start.23
  375.6 3.1 copy-start.13
  375.6 3.1 copy-start.14
  406.6 1.2 copy-start.7
  406.6 1.5 copy-start.8
  408.1 1.2 copy-start.3
  408.1 1.5 copy-start.4
  409.7 1.2 copy-start
  411.1 6.4 %copy-start.22 = (s32[16,128]{1,0:T(8,128)S(1)}, s32[16,128]{1,0:T(8,128)}, u32[]{:S(2)}) copy-start(s32[16,128]{1,0:T(8,128)} %get-tuple-element.143) | copy-start | bytes 24580
  442.3 45.7 %copy-start.12 = (f32[1,2,256,128]{2,3,1,0:T(8,128)S(1)}, f32[1,2,256,128]{2,3,1,0:T(8,128)}, u32[]{:S(2)}) copy-start(f32[1,2,256,128]{2,3,1,0:T(8,128)} %copy-done.11) | copy-start | bytes 786436
  442.3 45.7 %copy-start.17 = (f32[1,2,256,128]{2,3,1,0:T(8,128)S(1)}, f32[1,2,256,128]{2,3,1,0:T(8,128)}, u32[]{:S(2)}) copy-start(f32[1,2,256,128]{2,3,1,0:T(8,128)} %reduce-scatter.3.cloned.1.call-done) | copy-start | bytes 786436
  442.3 10.9 %collective-permute-start.3 = (f32[4,2,256,128]{2,3,1,0:T(8,128)S(1)}, f32[4,2,256,128]{2,3,1,0:T(8,128)S(1)}, u32[]{:S(2)}, u32[]{:S(2)}) collective-permute-start(f32[4,2,256,128]{2,3,1,0:T(8,128)S(1)} %slice.507), channel_id=1, source_target_pairs={{0,4},{4,8},{8,12},{12,16},{16,20},{20,24},{24,28},{28,32},{32,36}... | collective-permute-start | bytes 3145736 | tf_op jit(solution)/shard_map/ppermute | solution.py:15
  (1 other events, 0.7 us)
Sparse Core Ops, SparseCore 0:
  246.5 35.0 reduce-scatter.2
  454.5 33.4 reduce-scatter.4
